TPU v7x, 32 devices: a whole 2x2x4 slice. The times are simulated.
32 devices in a mesh: aux: 4 (over y, x), blk: 8 (over z, core).
Axes of the slice: x: 2, y: 2, z: 4, core: 2. Of those that a mesh axis runs over, the one named last changes fastest.
Arguments:
- integrals: bfloat16 [2048, 64, 1024], P(('aux', 'blk')), may hold values from -0.5 to 0.5
- metric: bfloat16 [2048, 512], P('aux'), may hold values from -1 to 2
- pair_list: int32 [15, 2], replicated, may hold values from 0 to 7, as said below
- aux_mask: int32 [16, 8], P('aux'), may hold values 0 or 1
Outputs:
- band_rows: float32 [8, 128, 640], P('blk', 'aux')
Inputs may be any that keep to these rules, and one draw needn't show every extreme that they name: `pair_list`: every pair (r, r) appears once; the other rows are distinct pairs (r, r + 1) or (r, r + 2) with both blocks below 8; 7 such rows.
All inputs are finite; a program needn't handle non-finite values. No bound on the sum of `aux_mask` on one device may be relied on, other than what follows from the above.
Results may differ from a plain program's by a relative error of at most 0.0015.
Values may be sent and summed in bfloat16 or wider, within the bound.
A program may use at most 128 MiB of HBM per device.

v0:
```python
import jax
import jax.numpy as jnp
from jax import lax
from jax.sharding import PartitionSpec as P

BS = 128
QB = 128
SPAN = 3


def from_behind(array, axis, by):
    peers = lax.axis_size(axis)
    pairs = [(i, i + by) for i in range(peers) if 0 <= i + by < peers]
    return lax.ppermute(array, axis, pairs)


def fit_block(metric, slab_piece, mask_rows):
    fitted = jnp.einsum("pq,qjn->pjn", metric, slab_piece, preferred_element_type=jnp.float32)
    return (fitted * mask_rows[:, None, None]).astype(jnp.bfloat16)


def local(integrals, metric, pair_list, aux_mask):
    block_count = aux_mask.shape[1]
    position = lax.axis_index("blk")
    block_ids = jnp.arange(block_count, dtype=jnp.int32)
    offsets = jnp.arange(SPAN, dtype=jnp.int32)
    col_gap = pair_list[:, 1] - pair_list[:, 0]
    hits = (pair_list[:, 0][:, None] == position) & (col_gap[:, None] == offsets[None, :])
    listed = jnp.sum(hits.astype(jnp.int32), axis=0)
    one_hot = (block_ids == position).astype(jnp.int32)
    column = jnp.sum(aux_mask * one_hot[None, :], axis=1)
    own_mask = jnp.repeat(column, QB).astype(jnp.float32)
    own_block = fit_block(
        metric, lax.all_to_all(integrals, "blk", split_axis=2, concat_axis=0, tiled=True), own_mask
    )
    partners = [own_block]
    current = own_block
    for turn_index in range(SPAN - 1):
        current = from_behind(current, "blk", -1)
        partners.append(current)
    flat_own = partners[0].reshape(-1, BS)

    def make_tile(partner):
        return lax.dot_general(
            flat_own,
            partner.reshape(-1, BS),
            (((0,), (0,)), ((), ())),
            preferred_element_type=jnp.float32,
        )

    tile_list = [
        make_tile(partners[offset]) * listed[offset].astype(jnp.float32) for offset in range(SPAN)
    ]
    upper_tiles = jnp.stack(tile_list)
    mirror_tiles = jnp.stack([jnp.transpose(tile_list[offset]) for offset in range(1, SPAN)])
    lower_tiles = []
    moving = mirror_tiles
    for turn_index in range(SPAN - 1):
        moving = from_behind(moving.astype(jnp.bfloat16), "blk", 1).astype(moving.dtype)
        lower_tiles.append(moving[0])
        moving = moving[1:]
    whole_band = jnp.concatenate(
        [jnp.stack([lower_tiles[SPAN - 2 - slot] for slot in range(SPAN - 1)]), upper_tiles], axis=0
    )
    band_parts = lax.psum_scatter(whole_band, "aux", scatter_dimension=1, tiled=True)
    pieces = [band_parts[slot] for slot in range(2 * SPAN - 1)]
    band_rows = jnp.concatenate(pieces, axis=1)
    return band_rows[None]


def solution(mesh):
    return jax.shard_map(
        local,
        mesh=mesh,
        in_specs=(P(("aux", "blk"), None, None), P("aux", None), P(), P("aux", None)),
        out_specs=P("blk", "aux", None),
        check_vma=False,
    )
```

profile of v0, /device:TPU:0, one launch (start us, length us, event | category | flops | bytes accessed | tf_op | source)
XLA Modules:
  0.0 535.0 jit_solution(6103885854642759354)
XLA Ops:
  6.5 0.0 copy-start
  6.5 24.0 %copy.18 = bf16[64,64,1024]{1,0,2:T(8,128)(2,1)} copy(bf16[64,64,1024]{2,1,0:T(8,128)(2,1)} %param.4) | data formatting | bytes 16777216 | tf_op args[0]
  30.5 16.9 %reshape.23 = bf16[8,2,262144]{2,1,0:T(2,128)(2,1)} reshape(bf16[1024,64,64]{2,1,0:T(8,128)(2,1)} %bitcast.79) | data formatting | bytes 16777216
  47.4 0.0 copy-start.4
  47.4 6.5 %all-to-all-start = ((bf16[8,2,262144]{2,1,0:T(2,128)(2,1)}), bf16[8,2,262144]{2,1,0:T(2,128)(2,1)}, u32[]{:S(2)}, u32[]{:S(2)}) async-start(bf16[8,2,262144]{2,1,0:T(2,128)(2,1)} %reshape.23), calls=%async_computation | async-start | bytes 16777216 | tf_op jit(solution)/shard_map/all_to_all | solution.py:34
  53.9 0.0 reduce-scatter.2.cloned.1.call-start
  54.0 0.0 copy-done.4
  54.0 0.1 multiply_reduce_fusion
  54.1 0.1 broadcast_bitcast_fusion
  54.2 183.7 %all-to-all-done = bf16[8,2,262144]{2,1,0:T(2,128)(2,1)} async-done(((bf16[8,2,262144]{2,1,0:T(2,128)(2,1)}), bf16[8,2,262144]{2,1,0:T(2,128)(2,1)}, u32[]{:S(2)}, u32[]{:S(2)}) %all-to-all-start) | async-done | bytes 8388640 | tf_op jit(solution)/shard_map/all_to_all | solution.py:34
  237.9 16.5 %reshape.24 = bf16[1024,64,64]{2,1,0:T(8,128)(2,1)} reshape(bf16[8,2,262144]{2,1,0:T(2,128)(2,1)} %all-to-all-done) | data formatting | bytes 16777216
  254.3 27.7 %copy.19 = bf16[64,64,8,128]{3,0,2,1:T(8,128)(2,1)} copy(bf16[64,64,8,128]{1,0,3,2:T(8,128)(2,1)} %bitcast.78) | data formatting | bytes 16777216 | tf_op jit(solution)/shard_map/all_to_all | solution.py:34
  282.1 0.0 copy-done
  282.1 0.0 copy-start.5
  282.1 8.1 %multiply_convert_fusion = bf16[512,64,128]{2,0,1:T(8,128)(2,1)S(1)} fusion(bf16[512,64,128]{2,0,1:T(8,128)(2,1)} %bitcast.80, f32[512]{0:T(512)S(1)} %broadcast_bitcast_fusion, bf16[512,512]{1,0:T(8,128)(2,1)S(1)} %copy-done), kind=kOutput, calls=%fused_computation | convolution fusion | flops 4303355904 | bytes 17303552 | tf_op jit(solution)/shard_map/pq,qjn->pjn/dot_general | solution.py:18
  290.2 0.0 copy-start.1
  290.2 1.3 collective-permute-start
  291.5 13.8 %collective-permute-done = bf16[512,64,128]{2,0,1:T(8,128)(2,1)S(1)} collective-permute-done((bf16[512,64,128]{2,0,1:T(8,128)(2,1)S(1)}, bf16[512,64,128]{2,0,1:T(8,128)(2,1)S(1)}, u32[]{:S(2)}, u32[]{:S(2)}) %collective-permute-start) | collective-permute-done | bytes 8388640 | tf_op jit(solution)/shard_map/ppermute | solution.py:14
  305.3 1.5 collective-permute-start.1
  306.7 0.0 copy-done.5
  306.8 0.1 convert_reduce_fusion
  306.9 0.7 fusion.7
  308.9 2.5 fusion.4
  311.4 87.7 %collective-permute-done.1 = bf16[512,64,128]{2,0,1:T(8,128)(2,1)S(1)} collective-permute-done((bf16[512,64,128]{2,0,1:T(8,128)(2,1)S(1)}, bf16[512,64,128]{2,0,1:T(8,128)(2,1)S(1)}, u32[]{:S(2)}, u32[]{:S(2)}) %collective-permute-start.1) | collective-permute-done | bytes 8388640 | tf_op jit(solution)/shard_map/ppermute | solution.py:14
  399.1 0.0 copy-done.1
  399.1 2.4 fusion.3
  401.5 82.1 %collective-permute-start.2 = (bf16[2,128,128]{1,2,0:T(8,128)(2,1)S(1)}, bf16[2,128,128]{1,2,0:T(8,128)(2,1)S(1)}, u32[]{:S(2)}, u32[]{:S(2)}) collective-permute-start(bf16[2,128,128]{1,2,0:T(8,128)(2,1)S(1)} %pad_maximum_fusion), channel_id=1, source_target_pairs={{0,1},{1,2},{2,3},{3,4},{4,5},{5,6},{6,7},{8,9},{9,10},{10,11},{11... | collective-permute-start | bytes 196616 | tf_op jit(solution)/shard_map/ppermute | solution.py:14
  483.6 0.9 collective-permute-done.2
  484.5 2.3 collective-permute-start.3
  487.5 0.1 copy.24
  487.6 0.1 collective-permute-done.3
  487.7 0.1 copy.23
  487.8 8.2 %fusion.2 = f32[5,128,128]{2,1,0:T(8,128)S(1)} fusion(f32[5,128,128]{2,1,0:T(8,128)S(1)} %constant_dynamic-update-slice_fusion, bf16[512,64,128]{2,0,1:T(8,128)(2,1)} %copy-done.1, f32[]{:T(128)} %bitcast.16), kind=kOutput, calls=%fused_computation.4 | convolution fusion | flops 1073758208 | bytes 16843264 | tf_op jit(solution)/shard_map/dot_general | solution.py:44
  496.0 0.0 copy-start.2
  496.0 0.7 copy-done.2
  496.7 0.0 reduce-scatter.2.cloned.1.call-update
  496.8 27.1 %reduce-scatter.2.cloned.1.call-done = f32[5,32,128]{2,1,0:T(8,128)} async-done(((f32[5,128,128]{2,1,0:T(8,128)}), f32[5,32,128]{2,1,0:T(8,128)}) %reduce-scatter.2.cloned.1.call-update) | async-done | bytes 81936 | tf_op jit(solution)/shard_map/reduce_scatter | solution.py:65
  523.9 0.7 constant_dynamic-update-slice_fusion.6
  524.6 0.7 constant_dynamic-update-slice_fusion.5
  525.4 0.7 constant_dynamic-update-slice_fusion.4
  526.1 0.7 constant_dynamic-update-slice_fusion.3
  526.8 0.7 constant_dynamic-update-slice_fusion.2
  527.5 0.0 copy-start.3
  527.5 0.6 copy-done.3
  (12 shorter events, 0.1 us)
Async XLA Ops:
  6.5 275.5 %copy-start = (bf16[512,512]{1,0:T(8,128)(2,1)S(1)}, bf16[512,512]{1,0:T(8,128)(2,1)}, u32[]{:S(2)}) copy-start(bf16[512,512]{1,0:T(8,128)(2,1)} %param.5) | copy-start | bytes 1572868
  47.4 6.5 %copy-start.4 = (s32[4,8]{1,0:T(4,128)S(1)}, s32[4,8]{1,0:T(4,128)}, u32[]{:S(2)}) copy-start(s32[4,8]{1,0:T(4,128)} %param.7) | copy-start | bytes 388
  47.4 190.4 %all-to-all-start = ((bf16[8,2,262144]{2,1,0:T(2,128)(2,1)}), bf16[8,2,262144]{2,1,0:T(2,128)(2,1)}, u32[]{:S(2)}, u32[]{:S(2)}) async-start(bf16[8,2,262144]{2,1,0:T(2,128)(2,1)} %reshape.23), calls=%async_computation | async-start | bytes 16777216 | tf_op jit(solution)/shard_map/all_to_all | solution.py:34
  53.9 470.0 %reduce-scatter.2.cloned.1.call-start = ((), (), s32[]{:S(2)}) async-start(), calls=%async_computation.2 | async-start | bytes 409600 | tf_op jit(solution)/shard_map/reduce_scatter | solution.py:65
  282.1 24.7 %copy-start.5 = (s32[15,2]{0,1:T(2,128)S(1)}, s32[15,2]{0,1:T(2,128)}, u32[]{:S(2)}) copy-start(s32[15,2]{0,1:T(2,128)} %param.6) | copy-start | bytes 364
  290.2 108.9 %copy-start.1 = (bf16[512,64,128]{2,0,1:T(8,128)(2,1)}, bf16[512,64,128]{2,0,1:T(8,128)(2,1)S(1)}, u32[]{:S(2)}) copy-start(bf16[512,64,128]{2,0,1:T(8,128)(2,1)S(1)} %multiply_convert_fusion) | copy-start | bytes 25165828
  290.2 15.1 %collective-permute-start = (bf16[512,64,128]{2,0,1:T(8,128)(2,1)S(1)}, bf16[512,64,128]{2,0,1:T(8,128)(2,1)S(1)}, u32[]{:S(2)}, u32[]{:S(2)}) collective-permute-start(bf16[512,64,128]{2,0,1:T(8,128)(2,1)S(1)} %multiply_convert_fusion), channel_id=1, source_target_pairs={{1,0},{2,1},{3,2},{4,3},{5,4},{6,5},{7,6},{9,8},{10,9},{11,10},{12... | collective-permute-start | bytes 25165832 | tf_op jit(solution)/shard_map/ppermute | solution.py:14
  305.3 93.8 %collective-permute-start.1 = (bf16[512,64,128]{2,0,1:T(8,128)(2,1)S(1)}, bf16[512,64,128]{2,0,1:T(8,128)(2,1)S(1)}, u32[]{:S(2)}, u32[]{:S(2)}) collective-permute-start(bf16[512,64,128]{2,0,1:T(8,128)(2,1)S(1)} %collective-permute-done), channel_id=1, source_target_pairs={{1,0},{2,1},{3,2},{4,3},{5,4},{6,5},{7,6},{9,8},{10,9},{11,10},{12... | collective-permute-start | bytes 25165832 | tf_op jit(solution)/shard_map/ppermute | solution.py:14
  401.5 83.0 %collective-permute-start.2 = (bf16[2,128,128]{1,2,0:T(8,128)(2,1)S(1)}, bf16[2,128,128]{1,2,0:T(8,128)(2,1)S(1)}, u32[]{:S(2)}, u32[]{:S(2)}) collective-permute-start(bf16[2,128,128]{1,2,0:T(8,128)(2,1)S(1)} %pad_maximum_fusion), channel_id=1, source_target_pairs={{0,1},{1,2},{2,3},{3,4},{4,5},{5,6},{6,7},{8,9},{9,10},{10,11},{11... | collective-permute-start | bytes 196616 | tf_op jit(solution)/shard_map/ppermute | solution.py:14
  484.5 3.2 collective-permute-start.3
  496.0 0.7 copy-start.2
  527.5 0.6 copy-start.3
Sparse Core Ops, SparseCore 0:
  496.9 26.9 reduce-scatter.1
where the time goes:
time: 537 us; the launch traced here: 535 us
  waiting for transfers between devices  313 us (58%)
  starting transfers between devices  93.7 us (17%)
  local copies, waits for them, and re-layouts  91 us (17%)
  matrix products  21.2 us (4%)
  between operations  15.5 us (3%)
    all_to_all x1, waiting for transfers between devices, local(): lax.all_to_all(integrals, 'blk', split_axis=2, concat_axis=0, tiled=True)  184 us
    ppermute x4, waiting for transfers between devices, from_behind(): return lax.ppermute(array, axis, pairs)  102 us
    ppermute x4, starting transfers between devices, from_behind(): return lax.ppermute(array, axis, pairs)  87.2 us
    unnamed x22, local copies, waits for them, and re-layouts  61.6 us
    all_to_all x1, local copies, waits for them, and re-layouts, local(): lax.all_to_all(integrals, 'blk', split_axis=2, concat_axis=0, tiled=True)  27.7 us
    reduce_scatter x1, waiting for transfers between devices, local(): lax.psum_scatter(whole_band, 'aux', scatter_dimension=1, tiled=True)  27.1 us
    dot_general x3, matrix products, make_tile(): lax.dot_general(flat_own, partner.reshape(-1, BS), (((0,), (0,)), ((), ()...  13.1 us
  transfers between devices with their start and end apart: 6, of which 6 were waited for; matrix products, arithmetic and copies ran while one was open for 1% of the time, Pallas kernels for 0%

commit v1 on v0

--- a/solution.py
+++ b/solution.py
@@ -31,7 +31,14 @@
     column = jnp.sum(aux_mask * one_hot[None, :], axis=1)
     own_mask = jnp.repeat(column, QB).astype(jnp.float32)
     own_block = fit_block(
-        metric, lax.all_to_all(integrals, "blk", split_axis=2, concat_axis=0, tiled=True), own_mask
+        metric,
+        jnp.concatenate(
+            lax.all_to_all(
+                jnp.stack(jnp.split(integrals, lax.axis_size("blk"), axis=2)), "blk", 0, 0
+            ),
+            axis=0,
+        ),
+        own_mask,
     )
     partners = [own_block]
     current = own_block

time: 537 us -> 503 us (0.937)
  local copies, waits for them, and re-layouts: 91 us -> 24.3 us
  matrix products: 21.2 us -> 57.2 us
    unnamed x22 -> x26, local copies, waits for them, and re-layouts: 61.6 us -> 20.4 us
    dot_general x1, matrix products: 8.13 us -> 37.7 us  [fit_block(): jnp.einsum('pq,qjn->pjn', metric, slab_piece, preferred_element_type=jnp....]
    all_to_all x1 -> x0, local copies, waits for them, and re-layouts: 27.7 us -> none  [local(): lax.all_to_all(integrals, 'blk', split_axis=2, concat_axis=0, tiled=True)]
    dot_general x3, matrix products: 13.1 us -> 19.5 us  [make_tile(): lax.dot_general(flat_own, partner.reshape(-1, BS), (((0,), (0,)), ((), ()...]
where the time goes in v1:
time: 503 us; the launch traced here: 502 us
  waiting for transfers between devices  311 us (62%)
  starting transfers between devices  93.5 us (19%)
  matrix products  57.2 us (11%)
  local copies, waits for them, and re-layouts  24.3 us (5%)
  between operations  15.6 us (3%)
    all_to_all x1, waiting for transfers between devices, local(): lax.all_to_all(jnp.stack(jnp.split(integrals, lax.axis_size('blk'), axis=...  184 us
    ppermute x4, waiting for transfers between devices, from_behind(): return lax.ppermute(array, axis, pairs)  99.8 us
    ppermute x4, starting transfers between devices, from_behind(): return lax.ppermute(array, axis, pairs)  87 us
    dot_general x1, matrix products, fit_block(): jnp.einsum('pq,qjn->pjn', metric, slab_piece, preferred_element_type=jnp....  37.7 us
    reduce_scatter x1, waiting for transfers between devices, local(): lax.psum_scatter(whole_band, 'aux', scatter_dimension=1, tiled=True)  27.2 us
    unnamed x26, local copies, waits for them, and re-layouts  20.4 us
    dot_general x3, matrix products, make_tile(): lax.dot_general(flat_own, partner.reshape(-1, BS), (((0,), (0,)), ((), ()...  19.5 us
  transfers between devices with their start and end apart: 6, of which 6 were waited for; matrix products, arithmetic and copies ran while one was open for 1% of the time, Pallas kernels for 0%

profile of v1, /device:TPU:0, one launch (start us, length us, event | category | flops | bytes accessed | tf_op | source)
XLA Modules:
  0.0 501.5 jit_solution(6617565357518721746)
XLA Ops:
  6.5 0.0 copy-start
  6.5 2.4 bitcast_dynamic-update-slice_fusion.7
  8.9 2.2 bitcast_dynamic-update-slice_fusion.6
  11.2 2.3 bitcast_dynamic-update-slice_fusion.5
  13.5 2.3 bitcast_dynamic-update-slice_fusion.4
  15.8 2.3 bitcast_dynamic-update-slice_fusion.3
  18.1 2.3 bitcast_dynamic-update-slice_fusion.2
  20.4 2.3 bitcast_dynamic-update-slice_fusion.1
  22.6 2.3 bitcast_dynamic-update-slice_fusion
  24.9 0.0 copy-start.4
  24.9 6.5 %all-to-all-start = ((bf16[8,64,64,128]{3,2,1,0:T(8,128)(2,1)}), bf16[8,64,64,128]{3,2,1,0:T(8,128)(2,1)}, u32[]{:S(2)}, u32[]{:S(2)}) async-start(bf16[8,64,64,128]{3,2,1,0:T(8,128)(2,1)} %bitcast_dynamic-update-slice_fusion), calls=%async_computation | async-start | bytes 16777216 | tf_op jit(solution)/shard_map/all_to_all | solution.py:36
  31.4 0.0 reduce-scatter.2.cloned.1.call-start
  31.5 0.0 copy-done.4
  31.5 0.1 multiply_reduce_fusion
  31.6 0.1 broadcast_bitcast_fusion
  31.7 183.7 %all-to-all-done = bf16[8,64,64,128]{3,2,1,0:T(8,128)(2,1)} async-done(((bf16[8,64,64,128]{3,2,1,0:T(8,128)(2,1)}), bf16[8,64,64,128]{3,2,1,0:T(8,128)(2,1)}, u32[]{:S(2)}, u32[]{:S(2)}) %all-to-all-start) | async-done | bytes 8388640 | tf_op jit(solution)/shard_map/all_to_all | solution.py:36
  215.4 0.0 copy-done
  215.4 0.0 copy-start.5
  215.4 37.7 %fusion.1 = bf16[512,64,128]{0,2,1:T(8,128)(2,1)S(1)} fusion(f32[512]{0:T(512)S(1)} %broadcast_bitcast_fusion, bf16[512,64,128]{2,1,0:T(8,128)(2,1)} %bitcast.8, bf16[512,512]{1,0:T(8,128)(2,1)S(1)} %copy-done), kind=kOutput, calls=%fused_computation.2 | convolution fusion | flops 4303355904 | bytes 17303552 | tf_op jit(solution)/shard_map/pq,qjn->pjn/dot_general | solution.py:18
  253.1 0.0 copy-start.1
  253.1 1.3 collective-permute-start
  254.4 13.9 %collective-permute-done = bf16[512,64,128]{0,2,1:T(8,128)(2,1)} collective-permute-done((bf16[512,64,128]{0,2,1:T(8,128)(2,1)S(1)}, bf16[512,64,128]{0,2,1:T(8,128)(2,1)}, u32[]{:S(2)}, u32[]{:S(2)}) %collective-permute-start) | collective-permute-done | bytes 8388640 | tf_op jit(solution)/shard_map/ppermute | solution.py:14
  268.3 1.3 collective-permute-start.1
  269.6 0.0 copy-done.5
  269.6 0.1 convert_reduce_fusion
  269.7 0.7 fusion.11
  271.7 5.7 %fusion.8 = f32[128,128]{1,0:T(8,128)S(1)} fusion(bf16[512,64,128]{0,2,1:T(8,128)(2,1)S(1)} %fusion.1, bf16[512,64,128]{0,2,1:T(8,128)(2,1)} %collective-permute-done, f32[]{:T(128)} %bitcast.15), kind=kOutput, calls=%fused_computation.10 | convolution fusion | flops 1073758208 | bytes 16842756 | tf_op jit(solution)/shard_map/dot_general | solution.py:51
  277.4 85.0 %collective-permute-done.1 = bf16[512,64,128]{0,2,1:T(8,128)(2,1)} collective-permute-done((bf16[512,64,128]{0,2,1:T(8,128)(2,1)}, bf16[512,64,128]{0,2,1:T(8,128)(2,1)}, u32[]{:S(2)}, u32[]{:S(2)}) %collective-permute-start.1) | collective-permute-done | bytes 8388640 | tf_op jit(solution)/shard_map/ppermute | solution.py:14
  362.4 0.0 copy-done.1
  362.4 5.7 %fusion.7 = f32[128,128]{1,0:T(8,128)S(1)} fusion(bf16[512,64,128]{0,2,1:T(8,128)(2,1)S(1)} %fusion.1, bf16[512,64,128]{0,2,1:T(8,128)(2,1)} %collective-permute-done.1, f32[]{:T(128)} %bitcast.19), kind=kOutput, calls=%fused_computation.8 | convolution fusion | flops 1073758208 | bytes 16842756 | tf_op jit(solution)/shard_map/dot_general | solution.py:51
  368.1 82.1 %collective-permute-start.2 = (bf16[2,128,128]{1,2,0:T(8,128)(2,1)S(1)}, bf16[2,128,128]{1,2,0:T(8,128)(2,1)S(1)}, u32[]{:S(2)}, u32[]{:S(2)}) collective-permute-start(bf16[2,128,128]{1,2,0:T(8,128)(2,1)S(1)} %pad_maximum_fusion), channel_id=1, source_target_pairs={{0,1},{1,2},{2,3},{3,4},{4,5},{5,6},{6,7},{8,9},{9,10},{10,11},{11... | collective-permute-start | bytes 196616 | tf_op jit(solution)/shard_map/ppermute | solution.py:14
  450.2 0.9 collective-permute-done.2
  451.1 2.3 collective-permute-start.3
  454.1 0.1 copy.22
  454.2 0.1 collective-permute-done.3
  454.3 0.1 copy.21
  454.4 8.1 %fusion.6 = f32[5,128,128]{2,1,0:T(8,128)S(1)} fusion(f32[5,128,128]{2,1,0:T(8,128)S(1)} %constant_dynamic-update-slice_fusion, bf16[512,64,128]{0,2,1:T(8,128)(2,1)} %copy-done.1, f32[]{:T(128)} %bitcast.23), kind=kOutput, calls=%fused_computation.6 | convolution fusion | flops 1073758208 | bytes 16843264 | tf_op jit(solution)/shard_map/dot_general | solution.py:51
  462.6 0.0 copy-start.2
  462.6 0.7 copy-done.2
  463.3 0.0 reduce-scatter.2.cloned.1.call-update
  463.3 27.2 %reduce-scatter.2.cloned.1.call-done = f32[5,32,128]{2,1,0:T(8,128)} async-done(((f32[5,128,128]{2,1,0:T(8,128)}), f32[5,32,128]{2,1,0:T(8,128)}) %reduce-scatter.2.cloned.1.call-update) | async-done | bytes 81936 | tf_op jit(solution)/shard_map/reduce_scatter | solution.py:72
  490.5 0.7 constant_dynamic-update-slice_fusion.6
  491.2 0.7 constant_dynamic-update-slice_fusion.5
  491.9 0.7 constant_dynamic-update-slice_fusion.4
  492.6 0.7 constant_dynamic-update-slice_fusion.3
  493.3 0.7 constant_dynamic-update-slice_fusion.2
  494.1 0.0 copy-start.3
  494.1 0.6 copy-done.3
  (12 shorter events, 0.1 us)
Async XLA Ops:
  6.5 208.8 %copy-start = (bf16[512,512]{1,0:T(8,128)(2,1)S(1)}, bf16[512,512]{1,0:T(8,128)(2,1)}, u32[]{:S(2)}) copy-start(bf16[512,512]{1,0:T(8,128)(2,1)} %param.5) | copy-start | bytes 1572868
  24.9 6.5 %copy-start.4 = (s32[4,8]{1,0:T(4,128)S(1)}, s32[4,8]{1,0:T(4,128)}, u32[]{:S(2)}) copy-start(s32[4,8]{1,0:T(4,128)} %param.7) | copy-start | bytes 388
  24.9 190.4 %all-to-all-start = ((bf16[8,64,64,128]{3,2,1,0:T(8,128)(2,1)}), bf16[8,64,64,128]{3,2,1,0:T(8,128)(2,1)}, u32[]{:S(2)}, u32[]{:S(2)}) async-start(bf16[8,64,64,128]{3,2,1,0:T(8,128)(2,1)} %bitcast_dynamic-update-slice_fusion), calls=%async_computation | async-start | bytes 16777216 | tf_op jit(solution)/shard_map/all_to_all | solution.py:36
  31.4 459.1 %reduce-scatter.2.cloned.1.call-start = ((), (), s32[]{:S(2)}) async-start(), calls=%async_computation.2 | async-start | bytes 409600 | tf_op jit(solution)/shard_map/reduce_scatter | solution.py:72
  215.4 54.2 %copy-start.5 = (s32[15,2]{0,1:T(2,128)S(1)}, s32[15,2]{0,1:T(2,128)}, u32[]{:S(2)}) copy-start(s32[15,2]{0,1:T(2,128)} %param.6) | copy-start | bytes 364
  253.1 109.3 %copy-start.1 = (bf16[512,64,128]{0,2,1:T(8,128)(2,1)}, bf16[512,64,128]{0,2,1:T(8,128)(2,1)S(1)}, u32[]{:S(2)}) copy-start(bf16[512,64,128]{0,2,1:T(8,128)(2,1)S(1)} %fusion.1) | copy-start | bytes 25165828
  253.1 15.2 %collective-permute-start = (bf16[512,64,128]{0,2,1:T(8,128)(2,1)S(1)}, bf16[512,64,128]{0,2,1:T(8,128)(2,1)}, u32[]{:S(2)}, u32[]{:S(2)}) collective-permute-start(bf16[512,64,128]{0,2,1:T(8,128)(2,1)S(1)} %fusion.1), channel_id=1, source_target_pairs={{1,0},{2,1},{3,2},{4,3},{5,4},{6,5},{7,6},{9,8},{10,9},{11,10},{12... | collective-permute-start | bytes 25165832 | tf_op jit(solution)/shard_map/ppermute | solution.py:14
  268.3 94.1 %collective-permute-start.1 = (bf16[512,64,128]{0,2,1:T(8,128)(2,1)}, bf16[512,64,128]{0,2,1:T(8,128)(2,1)}, u32[]{:S(2)}, u32[]{:S(2)}) collective-permute-start(bf16[512,64,128]{0,2,1:T(8,128)(2,1)} %collective-permute-done), channel_id=1, source_target_pairs={{1,0},{2,1},{3,2},{4,3},{5,4},{6,5},{7,6},{9,8},{10,9},{11,10},{12... | collective-permute-start | bytes 25165832 | tf_op jit(solution)/shard_map/ppermute | solution.py:14
  368.1 83.0 %collective-permute-start.2 = (bf16[2,128,128]{1,2,0:T(8,128)(2,1)S(1)}, bf16[2,128,128]{1,2,0:T(8,128)(2,1)S(1)}, u32[]{:S(2)}, u32[]{:S(2)}) collective-permute-start(bf16[2,128,128]{1,2,0:T(8,128)(2,1)S(1)} %pad_maximum_fusion), channel_id=1, source_target_pairs={{0,1},{1,2},{2,3},{3,4},{4,5},{5,6},{6,7},{8,9},{9,10},{10,11},{11... | collective-permute-start | bytes 196616 | tf_op jit(solution)/shard_map/ppermute | solution.py:14
  451.1 3.2 collective-permute-start.3
  462.6 0.7 copy-start.2
  494.1 0.6 copy-start.3
Sparse Core Ops, SparseCore 0:
  463.4 27.0 reduce-scatter.1
